TPU v7x, 512 devices: a whole 4x8x8 slice. The times are simulated.
512 devices in a mesh: seq: 32 (over y, x), head: 16 (over z, core).
Axes of the slice: x: 4, y: 8, z: 8, core: 2. Of those that a mesh axis runs over, the one named last changes fastest.
Arguments:
- queries: bfloat16 [8192, 8192], P('seq', 'head'), may hold values from -1.796875 to 1.796875
- key_rows: bfloat16 [8192, 8192], P('seq', 'head'), may hold values from -1.796875 to 1.796875
- value_rows: bfloat16 [8192, 8192], P('seq', 'head'), may hold values from -6 to 6
- level_table: float32 [64, 7, 64], P(None, None, 'head'), may hold values from 0.25 to 4
- level_index: int32 [8192, 7], P('seq'), may hold values from 0 to 63
- norm_gain: float32 [8192], replicated, may hold values from 0.5 to 1.5
- cotangent: bfloat16 [8192, 8192], P(('seq', 'head')), may hold values from -6 to 6
Outputs:
- normed: bfloat16 [8192, 8192], P(('seq', 'head'))
- grad_query: bfloat16 [8192, 8192], P('seq', 'head')
- grad_key: bfloat16 [8192, 8192], P('seq', 'head')
- grad_value: bfloat16 [8192, 8192], P('seq', 'head')
- grad_table: float32 [64, 7, 64], P(None, None, 'head')
- grad_gain: float32 [8192], replicated
All inputs are finite; a program needn't handle non-finite values.
Results may differ from a plain program's by a relative error of at most 0.014.
Values may be sent and summed in bfloat16 or wider, within the bound.
A program may use at most 64 MiB of HBM per device.

v0:
```python
import jax
import jax.numpy as jnp
from jax import lax
from jax.sharding import PartitionSpec as P

CH = 128
LEVELS = 7
TABLE = 64
EPSILON = 1e-06
HIGHEST = lax.Precision.HIGHEST


def swapped(value, axis, bit):
    mask = 2**bit
    pairs = [(source, source ^ mask) for source in range(lax.axis_size(axis))]
    return lax.ppermute(value, axis, pairs)


def bit_length_of(values, places):
    result = jnp.zeros_like(values)
    for exponent in range(places):
        result = result + (values >= 1 << exponent).astype(jnp.int32)
    return result


def level_mask(spans):
    row_ids = lax.broadcasted_iota(jnp.int32, (spans, spans), 0)
    col_ids = lax.broadcasted_iota(jnp.int32, (spans, spans), 1)
    lengths = bit_length_of(jnp.bitwise_xor(row_ids, col_ids), 16)
    stacked = [((lengths == 1) & (col_ids < row_ids)).astype(jnp.float32)]
    return jnp.stack(stacked)


def body(queries, key_rows, value_rows, level_table, level_index, norm_gain, cotangent):
    tok_dev = queries.shape[0]
    head_count = level_table.shape[2]
    head_width = queries.shape[1] // head_count
    spans = tok_dev // CH
    local_bits = spans.bit_length() - 1
    seq_bits = lax.axis_size("seq").bit_length() - 1
    cross_count = LEVELS - 1 - local_bits
    shard_id = lax.axis_index("seq")
    query_blocks = queries.reshape(spans, CH, head_count, head_width)
    key_blocks = key_rows.reshape(spans, CH, head_count, head_width)
    value_blocks = value_rows.reshape(spans, CH, head_count, head_width)
    onehot = (level_index[:, :, None] == jnp.arange(TABLE, dtype=jnp.int32)[None, None, :]).astype(
        jnp.float32
    )
    weights = jnp.einsum("tlx,xlh->tlh", onehot, level_table, precision=HIGHEST)
    weights = weights.reshape(spans, CH, LEVELS, head_count)
    span_states = jnp.einsum(
        "icha,ichb->ihab", key_blocks, value_blocks, preferred_element_type=jnp.float32
    )
    masks_local = level_mask(spans)
    intra_states = jnp.einsum("mij,jhab->imhab", masks_local, span_states, precision=HIGHEST)
    shard_total = jnp.sum(span_states, axis=0)
    state_zeros = jnp.zeros((cross_count, head_count, head_width, head_width), jnp.float32)
    shards_in = lax.all_gather(
        shard_total[None].astype(jnp.bfloat16), "seq", axis=0, tiled=True
    ).astype(jnp.float32)
    source = jnp.arange(shards_in.shape[0], dtype=jnp.int32)
    lengths = bit_length_of(jnp.bitwise_xor(source, shard_id), 16)
    slot_of = jnp.minimum(lengths + local_bits, LEVELS - 1) - local_bits - 1
    selector = (slot_of[:, None] == jnp.arange(cross_count, dtype=jnp.int32)[None, :]) & (
        source < shard_id
    )[:, None]
    cross_states = state_zeros + jnp.einsum(
        "sk,shab->khab", selector.astype(jnp.float32), shards_in, precision=HIGHEST
    )
    spread = jnp.broadcast_to(cross_states[None], (spans,) + cross_states.shape)
    level_states = jnp.concatenate([intra_states, spread], axis=1).astype(jnp.bfloat16)
    far_out = jnp.einsum(
        "icha,ilhab->iclhb", query_blocks, level_states, preferred_element_type=jnp.float32
    )
    row_ids = lax.broadcasted_iota(jnp.int32, (CH, CH), 0)
    col_ids = lax.broadcasted_iota(jnp.int32, (CH, CH), 1)
    causal = col_ids <= row_ids
    scores = jnp.einsum(
        "icha,inha->ihcn", query_blocks, key_blocks, preferred_element_type=jnp.float32
    )
    scores = jnp.where(causal, scores, 0.0)
    near_out = jnp.einsum(
        "ihcn,inhb->ichb",
        scores.astype(jnp.bfloat16),
        value_blocks,
        preferred_element_type=jnp.float32,
    )
    level_out = jnp.concatenate([near_out[:, :, None], far_out], axis=2)
    attn = jnp.sum(weights[..., None] * level_out, axis=2).astype(jnp.bfloat16)
    attn_rows = attn.reshape(tok_dev, head_count * head_width)
    token_attn = lax.all_to_all(attn_rows, "head", split_axis=0, concat_axis=1, tiled=True)
    attn_f = token_attn.astype(jnp.float32)
    inv_rms = lax.rsqrt(jnp.mean(attn_f * attn_f, axis=1, keepdims=True) + EPSILON)
    unit_rows = attn_f * inv_rms
    normed = (unit_rows * norm_gain).astype(jnp.bfloat16)
    grad_out = cotangent.astype(jnp.float32)
    scaled = grad_out * norm_gain
    grad_gain = lax.psum(jnp.sum(grad_out * unit_rows, axis=0), ("seq", "head"))
    grad_attn = (
        (scaled - unit_rows * jnp.mean(scaled * unit_rows, axis=1, keepdims=True)) * inv_rms
    ).astype(jnp.bfloat16)
    head_grad = lax.all_to_all(grad_attn, "head", split_axis=1, concat_axis=0, tiled=True)
    grad_blocks = head_grad.reshape(spans, CH, head_count, head_width)
    grad_f = grad_blocks.astype(jnp.float32)
    grad_weight = jnp.sum(level_out * grad_f[:, :, None], axis=4)
    along_values = jnp.einsum(
        "ichb,inhb->ihcn", grad_blocks, value_blocks, preferred_element_type=jnp.float32
    )
    first_weight = jnp.transpose(weights[:, :, 0, :], (0, 2, 1))[..., None]
    grad_scores = jnp.where(causal, along_values * first_weight, 0.0).astype(jnp.bfloat16)
    weighted_scores = jnp.where(causal, scores * first_weight, 0.0).astype(jnp.bfloat16)
    near_dq = jnp.einsum(
        "ihcn,inha->icha", grad_scores, key_blocks, preferred_element_type=jnp.float32
    )
    near_dk = jnp.einsum(
        "ihcn,icha->inha", grad_scores, query_blocks, preferred_element_type=jnp.float32
    )
    near_dv = jnp.einsum(
        "ihcn,ichb->inhb", weighted_scores, grad_blocks, preferred_element_type=jnp.float32
    )
    far_dq = jnp.einsum(
        "ichb,ilhab->iclha", grad_blocks, level_states, preferred_element_type=jnp.float32
    )
    grad_query = near_dq + jnp.sum(weights[:, :, 1:, :, None] * far_dq, axis=2)
    scaled_grad = (weights[:, :, 1:, :, None] * grad_f[:, :, None]).astype(jnp.bfloat16)
    query_grads = jnp.einsum(
        "icha,iclhb->ilhab", query_blocks, scaled_grad, preferred_element_type=jnp.float32
    )
    inner_grad = jnp.einsum(
        "mij,imhab->jhab", masks_local, query_grads[:, :local_bits], precision=HIGHEST
    )
    shard_grads = jnp.sum(query_grads[:, local_bits:], axis=0)
    cross_grad = jnp.zeros((head_count, head_width, head_width), jnp.float32)
    group_grads = shard_grads
    for bit_pos in range(seq_bits):
        partner = swapped(group_grads.astype(jnp.bfloat16), "seq", bit_pos).astype(
            group_grads.dtype
        )
        lower_half = 1.0 - jnp.bitwise_and(jnp.right_shift(shard_id, bit_pos), 1).astype(
            jnp.float32
        )
        level_slot = min(bit_pos, cross_count - 1)
        cross_grad = cross_grad + lower_half * partner[level_slot]
        group_grads = group_grads + partner
    key_state = (inner_grad + cross_grad[None]).astype(jnp.bfloat16)
    grad_key = near_dk + jnp.einsum(
        "jhab,jnhb->jnha", key_state, value_blocks, preferred_element_type=jnp.float32
    )
    grad_value = near_dv + jnp.einsum(
        "jhab,jnha->jnhb", key_state, key_blocks, preferred_element_type=jnp.float32
    )
    table_part = jnp.einsum(
        "tlx,tlh->xlh", onehot, grad_weight.reshape(tok_dev, LEVELS, head_count), precision=HIGHEST
    )
    grad_table = lax.psum(table_part, "seq")
    row_shape = (tok_dev, head_count * head_width)
    return (
        normed,
        grad_query.astype(jnp.bfloat16).reshape(row_shape),
        grad_key.astype(jnp.bfloat16).reshape(row_shape),
        grad_value.astype(jnp.bfloat16).reshape(row_shape),
        grad_table,
        grad_gain,
    )


def solution(mesh):
    placed = (
        P("seq", "head"),
        P("seq", "head"),
        P("seq", "head"),
        P(None, None, "head"),
        P("seq", None),
        P(),
        P(("seq", "head"), None),
    )
    return jax.shard_map(
        body,
        mesh=mesh,
        in_specs=placed,
        out_specs=(
            P(("seq", "head"), None),
            P("seq", "head"),
            P("seq", "head"),
            P("seq", "head"),
            P(None, None, "head"),
            P(),
        ),
        check_vma=False,
    )
```

profile of v0, /device:TPU:32, one launch (start us, length us, event | category | flops | bytes accessed | tf_op | source)
XLA Modules:
  0.0 519.8 jit_solution(9532326248119924726)
XLA Ops:
  7.2 1.1 reshape.150
  8.3 1.0 reshape.151
  9.3 0.9 fusion.135
  10.7 1.3 fusion.16
  12.6 0.8 copy-done.5
  13.8 86.5 %all-gather.3.cloned.1.call-done = bf16[128,128,128]{2,1,0:T(8,128)(2,1)} async-done(((bf16[4,128,128]{2,1,0:T(8,128)(2,1)}), bf16[128,128,128]{2,1,0:T(8,128)(2,1)}) %all-gather.3.cloned.1.call-update) | async-done | bytes 4194320 | tf_op jit(solution)/shard_map/all_gather | solution.py:58
  100.3 4.5 fusion.5
  104.8 0.6 copy.205
  105.8 1.0 copy-done.4
  106.8 0.6 convolution_bitcast_fusion.1
  107.4 1.7 copy-done.1
  109.1 0.5 multiply_reduce_fusion.1
  110.0 18.5 %all_to_all.26 = bf16[16,16,512]{2,1,0:T(8,128)(2,1)S(1)} all-to-all(bf16[16,16,512]{2,1,0:T(8,128)(2,1)S(1)} %convert_element_type.402), channel_id=1, replica_groups=mesh['seq'=32,'head'=16] {'head'}, dimensions={0} | all-to-all | bytes 524288 | tf_op jit(solution)/shard_map/all_to_all | solution.py:91
  128.8 0.4 fusion.22
  129.1 0.9 fusion.21
  130.0 0.7 copy.311
  130.7 3.5 all-to-all-start.1
  134.3 11.3 %all-to-all-done.1 = bf16[16,16,512]{2,0,1:T(8,128)(2,1)S(1)} async-done(((bf16[16,16,512]{2,0,1:T(8,128)(2,1)}), bf16[16,16,512]{2,0,1:T(8,128)(2,1)S(1)}, u32[]{:S(2)}, u32[]{:S(2)}) %all-to-all-start.1) | async-done | bytes 262176 | tf_op jit(solution)/shard_map/all_to_all | solution.py:102
  145.7 0.7 copy-done.10
  146.7 0.6 convolution_bitcast_fusion
  147.7 1.4 copy-done.3
  149.2 2.8 collective-permute-start
  152.0 16.3 %collective-permute-done = bf16[5,4,128,128]{2,3,0,1:T(8,128)(2,1)S(1)} collective-permute-done((bf16[5,4,128,128]{2,3,0,1:T(8,128)(2,1)S(1)}, bf16[5,4,128,128]{2,3,0,1:T(8,128)(2,1)S(1)}, u32[]{:S(2)}, u32[]{:S(2)}) %collective-permute-start) | collective-permute-done | bytes 655392 | tf_op jit(solution)/shard_map/ppermute | solution.py:16
  168.4 1.0 fusion.56
  169.4 4.0 collective-permute-start.1
  173.4 16.0 %collective-permute-done.1 = bf16[5,4,128,128]{2,3,0,1:T(8,128)(2,1)S(1)} collective-permute-done((bf16[5,4,128,128]{2,3,0,1:T(8,128)(2,1)}, bf16[5,4,128,128]{2,3,0,1:T(8,128)(2,1)S(1)}, u32[]{:S(2)}, u32[]{:S(2)}) %collective-permute-start.1) | collective-permute-done | bytes 655392 | tf_op jit(solution)/shard_map/ppermute | solution.py:16
  189.4 1.1 fusion.27
  190.5 4.0 collective-permute-start.2
  194.5 100.7 %psum.15 = f32[8192]{0:T(1024)} all-reduce(f32[8192]{0:T(1024)S(1)} %get-tuple-element.6), channel_id=1, replica_groups=mesh['seq'=32,'head'=16] {'seq','head'}, use_global_device_ids=true, to_apply=%region_9.10 | all-reduce | flops 8192 | bytes 65536 | tf_op jit(solution)/shard_map/psum | solution.py:98
  295.2 3.0 fusion.2
  298.2 2.0 copy.219
  300.3 1.3 fusion.11
  301.6 2.5 fusion.26
  304.0 2.5 collective-permute-start.3
  307.0 0.7 copy.310
  307.7 0.6 multiply_reduce_fusion
  308.4 1.9 slice_bitcast_fusion
  310.3 2.0 copy.226
  312.3 25.5 %collective-permute-done.3 = bf16[5,4,128,128]{2,3,0,1:T(8,128)(2,1)} collective-permute-done((bf16[5,4,128,128]{2,3,0,1:T(8,128)(2,1)}, bf16[5,4,128,128]{2,3,0,1:T(8,128)(2,1)}, u32[]{:S(2)}, u32[]{:S(2)}) %collective-permute-start.3) | collective-permute-done | bytes 655392 | tf_op jit(solution)/shard_map/ppermute | solution.py:16
  337.8 2.6 add_convert_fusion
  340.4 4.2 collective-permute-start.4
  344.9 157.1 %psum.14 = f32[64,7,4]{0,2,1:T(4,128)} all-reduce(f32[64,7,4]{0,2,1:T(4,128)S(1)} %convolution_bitcast_fusion.7), channel_id=1, replica_groups=mesh['seq'=32,'head'=16] {'seq'}, use_global_device_ids=true, to_apply=%region_7.8 | all-reduce | flops 1792 | bytes 14336 | tf_op jit(solution)/shard_map/psum | solution.py:155
  502.0 2.1 fusion.61
  504.1 2.4 fusion.28
  506.8 1.2 convert_element_type.422
  508.0 1.2 convert_element_type.425
  509.2 1.1 fusion.31
  512.1 0.9 copy_bitcast_fusion
  (79 shorter events, 5.9 us)
Async XLA Ops:
  7.2 3.1 copy-start
  7.2 3.1 copy-start.19
  7.2 3.4 copy-start.17
  7.2 93.1 %all-gather.3.cloned.1.call-start = ((), (), s32[]{:S(2)}) async-start(), calls=%async_computation.2 | async-start | bytes 4325376 | tf_op jit(solution)/shard_map/all_gather | solution.py:58
  12.2 93.5 %copy-start.15 = (bf16[2,1,4,128,128]{3,4,1,2,0:T(8,128)(2,1)}, bf16[2,1,4,128,128]{3,4,1,2,0:T(8,128)(2,1)S(1)}, u32[]{:S(2)}) copy-start(bf16[2,1,4,128,128]{3,4,1,2,0:T(8,128)(2,1)S(1)} %copy.206) | copy-start | bytes 786436
  12.6 0.8 copy-start.5
  13.8 93.6 %copy-start.6 = (f32[2,128,1,4,128]{1,4,2,3,0:T(8,128)}, f32[2,128,1,4,128]{1,4,2,3,0:T(8,128)S(1)}, u32[]{:S(2)}) copy-start(f32[2,128,1,4,128]{1,4,2,3,0:T(8,128)S(1)} %convolution_bitcast_fusion.5) | copy-start | bytes 1572868
  105.8 1.0 copy-start.4
  107.4 1.7 copy-start.1
  109.8 18.9 %copy-start.16 = (bf16[16,8192]{1,0:T(8,128)(2,1)S(1)}, bf16[16,8192]{1,0:T(8,128)(2,1)}, u32[]{:S(2)}) copy-start(bf16[16,8192]{1,0:T(8,128)(2,1)} %param.13) | copy-start | bytes 786436
  109.9 18.9 %copy-start.18 = (f32[8192]{0:T(1024)S(1)}, f32[8192]{0:T(1024)}, u32[]{:S(2)}) copy-start(f32[8192]{0:T(1024)} %param.12) | copy-start | bytes 98308
  130.7 14.9 %all-to-all-start.1 = ((bf16[16,16,512]{2,0,1:T(8,128)(2,1)}), bf16[16,16,512]{2,0,1:T(8,128)(2,1)S(1)}, u32[]{:S(2)}, u32[]{:S(2)}) async-start(bf16[16,16,512]{2,0,1:T(8,128)(2,1)} %bitcast.93), calls=%async_computation.1 | async-start | bytes 524288 | tf_op jit(solution)/shard_map/all_to_all | solution.py:102
  145.7 0.7 copy-start.10
  146.6 0.8 copy-start.8
  147.5 1.6 copy-start.3
  149.2 19.2 %collective-permute-start = (bf16[5,4,128,128]{2,3,0,1:T(8,128)(2,1)S(1)}, bf16[5,4,128,128]{2,3,0,1:T(8,128)(2,1)S(1)}, u32[]{:S(2)}, u32[]{:S(2)}) collective-permute-start(bf16[5,4,128,128]{2,3,0,1:T(8,128)(2,1)S(1)} %convert_element_type.415), channel_id=1, source_target_pairs={{0,16},{16,0},{32,48},{48,32},{64,80},{80,64},{96,112},{112,96},{1... | collective-permute-start | bytes 1966088 | tf_op jit(solution)/shard_map/ppermute | solution.py:16
  169.4 20.0 %collective-permute-start.1 = (bf16[5,4,128,128]{2,3,0,1:T(8,128)(2,1)}, bf16[5,4,128,128]{2,3,0,1:T(8,128)(2,1)S(1)}, u32[]{:S(2)}, u32[]{:S(2)}) collective-permute-start(bf16[5,4,128,128]{2,3,0,1:T(8,128)(2,1)} %fusion.56), channel_id=1, source_target_pairs={{0,32},{16,48},{32,0},{48,16},{64,96},{80,112},{96,64},{112,80},{1... | collective-permute-start | bytes 1966088 | tf_op jit(solution)/shard_map/ppermute | solution.py:16
  190.5 111.1 %collective-permute-start.2 = (bf16[5,4,128,128]{2,3,0,1:T(8,128)(2,1)}, bf16[5,4,128,128]{2,3,0,1:T(8,128)(2,1)}, u32[]{:S(2)}, u32[]{:S(2)}) collective-permute-start(bf16[5,4,128,128]{2,3,0,1:T(8,128)(2,1)} %fusion.27), channel_id=1, source_target_pairs={{0,64},{16,80},{32,96},{48,112},{64,0},{80,16},{96,32},{112,48},{1... | collective-permute-start | bytes 1966088 | tf_op jit(solution)/shard_map/ppermute | solution.py:16
  301.5 5.0 copy-start.13
  301.6 5.0 copy-start.12
  301.6 6.1 %copy-start.2 = (f32[2,128,6,4,128]{1,4,2,3,0:T(8,128)S(1)}, f32[2,128,6,4,128]{1,4,2,3,0:T(8,128)}, u32[]{:S(2)}) copy-start(f32[2,128,6,4,128]{1,4,2,3,0:T(8,128)} %copy-done.1) | copy-start | bytes 9437188
  304.0 3.7 copy-start.7
  304.0 3.7 copy-start.9
  304.0 33.8 %collective-permute-start.3 = (bf16[5,4,128,128]{2,3,0,1:T(8,128)(2,1)}, bf16[5,4,128,128]{2,3,0,1:T(8,128)(2,1)}, u32[]{:S(2)}, u32[]{:S(2)}) collective-permute-start(bf16[5,4,128,128]{2,3,0,1:T(8,128)(2,1)} %fusion.26), channel_id=1, source_target_pairs={{0,128},{16,144},{32,160},{48,176},{64,192},{80,208},{96,224},{112... | collective-permute-start | bytes 1966088 | tf_op jit(solution)/shard_map/ppermute | solution.py:16
  340.4 168.8 %collective-permute-start.4 = (bf16[5,4,128,128]{2,3,0,1:T(8,128)(2,1)}, bf16[5,4,128,128]{2,3,0,1:T(8,128)(2,1)}, u32[]{:S(2)}, u32[]{:S(2)}) collective-permute-start(bf16[5,4,128,128]{2,3,0,1:T(8,128)(2,1)} %add_convert_fusion), channel_id=1, source_target_pairs={{0,256},{16,272},{32,288},{48,304},{64,320},{80,336},{96,352},{112... | collective-permute-start | bytes 1966088 | tf_op jit(solution)/shard_map/ppermute | solution.py:16
  509.2 1.5 copy-start.11
  510.4 1.0 copy-start.14
Sparse Core Ops, SparseCore 0:
  11.8 88.4 all-gather.2
where the time goes:
time: 521 us; the launch traced here: 520 us
  blocking collectives  276 us (53%)
  waiting for transfers between devices  156 us (30%)
  starting transfers between devices  21.1 us (4%)
  local copies, waits for them, and re-layouts  19.3 us (4%)
  matrix products  19 us (4%)
  between operations  14.6 us (3%)
  other arithmetic  13.9 us (3%)
    psum x1, blocking collectives, body(): grad_table = lax.psum(table_part, 'seq')  157 us
    psum x1, blocking collectives, body(): grad_gain = lax.psum(jnp.sum(grad_out * unit_rows, axis=0), ('seq', 'head'))  101 us
    all_gather x1, waiting for transfers between devices, body(): lax.all_gather(shard_total[None].astype(jnp.bfloat16), 'seq', axis=0, til...  86.5 us
    ppermute x5, waiting for transfers between devices, swapped(): return lax.ppermute(value, axis, pairs)  57.8 us
    all_to_all x1, blocking collectives, body(): lax.all_to_all(attn_rows, 'head', split_axis=0, concat_axis=1, tiled=True)  18.5 us
    ppermute x5, starting transfers between devices, swapped(): return lax.ppermute(value, axis, pairs)  17.5 us
    all_to_all x1, waiting for transfers between devices, body(): lax.all_to_all(grad_attn, 'head', split_axis=1, concat_axis=0, tiled=True)  11.3 us
  transfers between devices with their start and end apart: 7, of which 5 were waited for; matrix products, arithmetic and copies ran while one was open for 4% of the time, Pallas kernels for 0%

commit v1 on v0

--- a/solution.py
+++ b/solution.py
@@ -95,7 +95,7 @@
     normed = (unit_rows * norm_gain).astype(jnp.bfloat16)
     grad_out = cotangent.astype(jnp.float32)
     scaled = grad_out * norm_gain
-    grad_gain = lax.psum(jnp.sum(grad_out * unit_rows, axis=0), ("seq", "head"))
+    grad_gain = lax.psum(lax.psum(jnp.sum(grad_out * unit_rows, axis=0), "seq"), "head")
     grad_attn = (
         (scaled - unit_rows * jnp.mean(scaled * unit_rows, axis=1, keepdims=True)) * inv_rms
     ).astype(jnp.bfloat16)

time: 521 us -> 470 us (0.902)
  blocking collectives: 276 us -> 220 us
  waiting for transfers between devices: 156 us -> 163 us
    psum x1, blocking collectives: 101 us -> 46.3 us  [body(): lax.psum(lax.psum(jnp.sum(grad_out * unit_rows, axis=0), 'seq'), 'head')]
    ppermute x5, waiting for transfers between devices: 57.8 us -> 64.9 us  [swapped(): return lax.ppermute(value, axis, pairs)]
  transfers between devices with their start and end apart: 7 -> 7, of which waited for: 5 -> 6; matrix products, arithmetic and copies ran while one was open for 4% -> 4% of each run, Pallas kernels for 0% -> 0%
where the time goes in v1:
time: 470 us; the launch traced here: 469 us
  blocking collectives  220 us (47%)
  waiting for transfers between devices  163 us (35%)
  starting transfers between devices  23.4 us (5%)
  local copies, waits for them, and re-layouts  19.5 us (4%)
  matrix products  15.5 us (3%)
  between operations  14.7 us (3%)
  other arithmetic  14.1 us (3%)
    psum x1, blocking collectives, body(): grad_table = lax.psum(table_part, 'seq')  155 us
    all_gather x1, waiting for transfers between devices, body(): lax.all_gather(shard_total[None].astype(jnp.bfloat16), 'seq', axis=0, til...  86.5 us
    ppermute x5, waiting for transfers between devices, swapped(): return lax.ppermute(value, axis, pairs)  64.9 us
    psum x1, blocking collectives, body(): lax.psum(lax.psum(jnp.sum(grad_out * unit_rows, axis=0), 'seq'), 'head')  46.3 us
    ppermute x5, starting transfers between devices, swapped(): return lax.ppermute(value, axis, pairs)  19.8 us
    all_to_all x1, blocking collectives, body(): lax.all_to_all(attn_rows, 'head', split_axis=0, concat_axis=1, tiled=True)  18.5 us
    all_to_all x1, waiting for transfers between devices, body(): lax.all_to_all(grad_attn, 'head', split_axis=1, concat_axis=0, tiled=True)  11.3 us
  transfers between devices with their start and end apart: 7, of which 6 were waited for; matrix products, arithmetic and copies ran while one was open for 4% of the time, Pallas kernels for 0%

profile of v1, /device:TPU:32, one launch (start us, length us, event | category | flops | bytes accessed | tf_op | source)
XLA Modules:
  0.0 469.5 jit_solution(18112285213449288374)
XLA Ops:
  7.2 1.1 reshape.150
  8.3 1.0 reshape.151
  9.3 0.9 fusion.135
  10.7 1.3 fusion.16
  12.6 0.8 copy-done.5
  13.8 86.5 %all-gather.3.cloned.1.call-done = bf16[128,128,128]{2,1,0:T(8,128)(2,1)} async-done(((bf16[4,128,128]{2,1,0:T(8,128)(2,1)}), bf16[128,128,128]{2,1,0:T(8,128)(2,1)}) %all-gather.3.cloned.1.call-update) | async-done | bytes 4194320 | tf_op jit(solution)/shard_map/all_gather | solution.py:58
  100.3 4.5 fusion.5
  104.8 0.6 copy.205
  105.8 1.0 copy-done.3
  106.8 0.6 convolution_bitcast_fusion.1
  107.4 1.7 copy-done.1
  109.1 0.5 multiply_reduce_fusion.1
  110.0 18.5 %all_to_all.26 = bf16[16,16,512]{2,1,0:T(8,128)(2,1)S(1)} all-to-all(bf16[16,16,512]{2,1,0:T(8,128)(2,1)S(1)} %convert_element_type.402), channel_id=1, replica_groups=mesh['seq'=32,'head'=16] {'head'}, dimensions={0} | all-to-all | bytes 524288 | tf_op jit(solution)/shard_map/all_to_all | solution.py:91
  128.7 0.4 fusion.22
  129.1 0.9 fusion.21
  130.0 0.7 copy.311
  130.7 3.5 all-to-all-start.1
  134.3 11.3 %all-to-all-done.1 = bf16[16,16,512]{2,0,1:T(8,128)(2,1)S(1)} async-done(((bf16[16,16,512]{2,0,1:T(8,128)(2,1)}), bf16[16,16,512]{2,0,1:T(8,128)(2,1)S(1)}, u32[]{:S(2)}, u32[]{:S(2)}) %all-to-all-start.1) | async-done | bytes 262176 | tf_op jit(solution)/shard_map/all_to_all | solution.py:102
  145.7 0.7 copy-done.11
  146.6 0.6 convolution_bitcast_fusion
  147.6 1.4 copy-done.2
  149.2 2.8 collective-permute-start
  152.0 16.3 %collective-permute-done = bf16[5,4,128,128]{2,3,0,1:T(8,128)(2,1)S(1)} collective-permute-done((bf16[5,4,128,128]{2,3,0,1:T(8,128)(2,1)S(1)}, bf16[5,4,128,128]{2,3,0,1:T(8,128)(2,1)S(1)}, u32[]{:S(2)}, u32[]{:S(2)}) %collective-permute-start) | collective-permute-done | bytes 655392 | tf_op jit(solution)/shard_map/ppermute | solution.py:16
  168.3 1.1 fusion.56
  169.4 4.0 collective-permute-start.1
  173.5 15.9 %collective-permute-done.1 = bf16[5,4,128,128]{2,3,0,1:T(8,128)(2,1)S(1)} collective-permute-done((bf16[5,4,128,128]{2,3,0,1:T(8,128)(2,1)}, bf16[5,4,128,128]{2,3,0,1:T(8,128)(2,1)S(1)}, u32[]{:S(2)}, u32[]{:S(2)}) %collective-permute-start.1) | collective-permute-done | bytes 655392 | tf_op jit(solution)/shard_map/ppermute | solution.py:16
  189.4 1.2 fusion.27
  190.5 4.2 collective-permute-start.2
  194.8 1.6 fusion.2
  196.4 2.1 copy.219
  198.4 2.7 multiply_reduce_fusion
  201.2 7.4 %collective-permute-done.2 = bf16[5,4,128,128]{2,3,0,1:T(8,128)(2,1)} collective-permute-done((bf16[5,4,128,128]{2,3,0,1:T(8,128)(2,1)}, bf16[5,4,128,128]{2,3,0,1:T(8,128)(2,1)}, u32[]{:S(2)}, u32[]{:S(2)}) %collective-permute-start.2) | collective-permute-done | bytes 655392 | tf_op jit(solution)/shard_map/ppermute | solution.py:16
  208.6 1.4 fusion.26
  210.1 4.0 collective-permute-start.3
  214.4 2.0 slice_bitcast_fusion
  216.7 25.2 %collective-permute-done.3 = bf16[5,4,128,128]{2,3,0,1:T(8,128)(2,1)S(1)} collective-permute-done((bf16[5,4,128,128]{2,3,0,1:T(8,128)(2,1)S(1)}, bf16[5,4,128,128]{2,3,0,1:T(8,128)(2,1)S(1)}, u32[]{:S(2)}, u32[]{:S(2)}) %collective-permute-start.3) | collective-permute-done | bytes 655392 | tf_op jit(solution)/shard_map/ppermute | solution.py:16
  241.9 2.7 add_convert_fusion
  244.6 4.8 %collective-permute-start.4 = (bf16[5,4,128,128]{2,3,0,1:T(8,128)(2,1)}, bf16[5,4,128,128]{2,3,0,1:T(8,128)(2,1)}, u32[]{:S(2)}, u32[]{:S(2)}) collective-permute-start(bf16[5,4,128,128]{2,3,0,1:T(8,128)(2,1)} %add_convert_fusion), channel_id=1, source_target_pairs={{0,256},{16,272},{32,288},{48,304},{64,320},{80,336},{96,352},{112... | collective-permute-start | bytes 1966088 | tf_op jit(solution)/shard_map/ppermute | solution.py:16
  249.9 0.7 copy.310
  250.7 2.0 copy.226
  252.7 154.9 %all-reduce = (f32[64,7,4]{0,2,1:T(4,128)}, f32[8192]{0:T(1024)S(1)}) all-reduce(f32[64,7,4]{0,2,1:T(4,128)S(1)} %convolution_bitcast_fusion.7, f32[8192]{0:T(1024)S(1)} %get-tuple-element.6), channel_id=1, replica_groups=mesh['seq'=32,'head'=16] {'seq'}, use_global_device_ids=true, to_apply=%region_7.8 | all-reduce | flops 9984 | bytes 79872 | tf_op jit(solution)/shard_map/psum | solution.py:155
  407.6 46.3 %psum.23 = f32[8192]{0:T(1024)} all-reduce(f32[8192]{0:T(1024)S(1)} %get-tuple-element.9), channel_id=1, replica_groups=mesh['seq'=32,'head'=16] {'head'}, use_global_device_ids=true, to_apply=%region_10.11 | all-reduce | flops 8192 | bytes 65536 | tf_op jit(solution)/shard_map/psum | solution.py:98
  453.8 2.1 fusion.61
  456.0 1.2 fusion.28
  457.5 1.3 convert_element_type.422
  458.9 1.1 fusion.31
  460.4 0.3 fusion.15
  461.8 0.9 copy_bitcast_fusion
  (89 shorter events, 6.0 us)
Async XLA Ops:
  7.2 3.1 copy-start
  7.2 3.1 copy-start.24
  7.2 3.4 copy-start.22
  7.2 93.1 %all-gather.3.cloned.1.call-start = ((), (), s32[]{:S(2)}) async-start(), calls=%async_computation.2 | async-start | bytes 4325376 | tf_op jit(solution)/shard_map/all_gather | solution.py:58
  12.2 93.5 %copy-start.19 = (bf16[2,1,4,128,128]{3,4,1,2,0:T(8,128)(2,1)}, bf16[2,1,4,128,128]{3,4,1,2,0:T(8,128)(2,1)S(1)}, u32[]{:S(2)}) copy-start(bf16[2,1,4,128,128]{3,4,1,2,0:T(8,128)(2,1)S(1)} %copy.206) | copy-start | bytes 786436
  12.6 0.9 copy-start.5
  13.8 93.6 %copy-start.7 = (f32[2,128,1,4,128]{1,4,2,3,0:T(8,128)}, f32[2,128,1,4,128]{1,4,2,3,0:T(8,128)S(1)}, u32[]{:S(2)}) copy-start(f32[2,128,1,4,128]{1,4,2,3,0:T(8,128)S(1)} %convolution_bitcast_fusion.5) | copy-start | bytes 1572868
  105.8 1.1 copy-start.3
  107.4 1.7 copy-start.1
  109.8 18.9 %copy-start.21 = (bf16[16,8192]{1,0:T(8,128)(2,1)S(1)}, bf16[16,8192]{1,0:T(8,128)(2,1)}, u32[]{:S(2)}) copy-start(bf16[16,8192]{1,0:T(8,128)(2,1)} %param.13) | copy-start | bytes 786436
  109.8 18.9 %copy-start.23 = (f32[8192]{0:T(1024)S(1)}, f32[8192]{0:T(1024)}, u32[]{:S(2)}) copy-start(f32[8192]{0:T(1024)} %param.12) | copy-start | bytes 98308
  130.7 14.9 %all-to-all-start.1 = ((bf16[16,16,512]{2,0,1:T(8,128)(2,1)}), bf16[16,16,512]{2,0,1:T(8,128)(2,1)S(1)}, u32[]{:S(2)}, u32[]{:S(2)}) async-start(bf16[16,16,512]{2,0,1:T(8,128)(2,1)} %bitcast.93), calls=%async_computation.1 | async-start | bytes 524288 | tf_op jit(solution)/shard_map/all_to_all | solution.py:102
  145.7 0.7 copy-start.11
  146.6 0.8 copy-start.8
  147.4 1.6 copy-start.2
  149.2 19.2 %collective-permute-start = (bf16[5,4,128,128]{2,3,0,1:T(8,128)(2,1)S(1)}, bf16[5,4,128,128]{2,3,0,1:T(8,128)(2,1)S(1)}, u32[]{:S(2)}, u32[]{:S(2)}) collective-permute-start(bf16[5,4,128,128]{2,3,0,1:T(8,128)(2,1)S(1)} %convert_element_type.415), channel_id=1, source_target_pairs={{0,16},{16,0},{32,48},{48,32},{64,80},{80,64},{96,112},{112,96},{1... | collective-permute-start | bytes 1966088 | tf_op jit(solution)/shard_map/ppermute | solution.py:16
  169.4 20.0 %collective-permute-start.1 = (bf16[5,4,128,128]{2,3,0,1:T(8,128)(2,1)}, bf16[5,4,128,128]{2,3,0,1:T(8,128)(2,1)S(1)}, u32[]{:S(2)}, u32[]{:S(2)}) collective-permute-start(bf16[5,4,128,128]{2,3,0,1:T(8,128)(2,1)} %fusion.56), channel_id=1, source_target_pairs={{0,32},{16,48},{32,0},{48,16},{64,96},{80,112},{96,64},{112,80},{1... | collective-permute-start | bytes 1966088 | tf_op jit(solution)/shard_map/ppermute | solution.py:16
  173.4 21.3 %copy-start.4 = (bf16[2,5,4,128,128]{3,4,1,2,0:T(8,128)(2,1)S(1)}, bf16[2,5,4,128,128]{3,4,1,2,0:T(8,128)(2,1)}, u32[]{:S(2)}) copy-start(bf16[2,5,4,128,128]{3,4,1,2,0:T(8,128)(2,1)} %copy-done.3) | copy-start | bytes 3932164
  173.4 21.3 %copy-start.12 = (bf16[2,128,4,128]{3,2,1,0:T(4,128)(2,1)S(1)}, bf16[2,128,4,128]{3,2,1,0:T(4,128)(2,1)}, u32[]{:S(2)}) copy-start(bf16[2,128,4,128]{3,2,1,0:T(4,128)(2,1)} %copy-done.11) | copy-start | bytes 786436
  173.5 21.3 %copy-start.20 = (bf16[2,1,4,128,128]{3,4,1,2,0:T(8,128)(2,1)S(1)}, bf16[2,1,4,128,128]{3,4,1,2,0:T(8,128)(2,1)}, u32[]{:S(2)}) copy-start(bf16[2,1,4,128,128]{3,4,1,2,0:T(8,128)(2,1)} %copy-done.19) | copy-start | bytes 786436
  190.5 18.1 %collective-permute-start.2 = (bf16[5,4,128,128]{2,3,0,1:T(8,128)(2,1)}, bf16[5,4,128,128]{2,3,0,1:T(8,128)(2,1)}, u32[]{:S(2)}, u32[]{:S(2)}) collective-permute-start(bf16[5,4,128,128]{2,3,0,1:T(8,128)(2,1)} %fusion.27), channel_id=1, source_target_pairs={{0,64},{16,80},{32,96},{48,112},{64,0},{80,16},{96,32},{112,48},{1... | collective-permute-start | bytes 1966088 | tf_op jit(solution)/shard_map/ppermute | solution.py:16
  201.2 12.9 %copy-start.13 = (bf16[2,128,4,128]{3,2,1,0:T(4,128)(2,1)S(1)}, bf16[2,128,4,128]{3,2,1,0:T(4,128)(2,1)}, u32[]{:S(2)}) copy-start(bf16[2,128,4,128]{3,2,1,0:T(4,128)(2,1)} %copy-done.11) | copy-start | bytes 786436
  210.1 6.4 %copy-start.16 = (f32[2,128,4,128]{3,1,2,0:T(8,128)S(1)}, f32[2,128,4,128]{3,1,2,0:T(8,128)}, u32[]{:S(2)}) copy-start(f32[2,128,4,128]{3,1,2,0:T(8,128)} %copy.219) | copy-start | bytes 1572868
  210.1 31.9 %collective-permute-start.3 = (bf16[5,4,128,128]{2,3,0,1:T(8,128)(2,1)S(1)}, bf16[5,4,128,128]{2,3,0,1:T(8,128)(2,1)S(1)}, u32[]{:S(2)}, u32[]{:S(2)}) collective-permute-start(bf16[5,4,128,128]{2,3,0,1:T(8,128)(2,1)S(1)} %fusion.26), channel_id=1, source_target_pairs={{0,128},{16,144},{32,160},{48,176},{64,192},{80,208},{96,224},{112... | collective-permute-start | bytes 1966088 | tf_op jit(solution)/shard_map/ppermute | solution.py:16
  214.4 2.3 copy-start.17
  241.9 2.7 copy-start.9
  244.6 214.3 %collective-permute-start.4 = (bf16[5,4,128,128]{2,3,0,1:T(8,128)(2,1)}, bf16[5,4,128,128]{2,3,0,1:T(8,128)(2,1)}, u32[]{:S(2)}, u32[]{:S(2)}) collective-permute-start(bf16[5,4,128,128]{2,3,0,1:T(8,128)(2,1)} %add_convert_fusion), channel_id=1, source_target_pairs={{0,256},{16,272},{32,288},{48,304},{64,320},{80,336},{96,352},{112... | collective-permute-start | bytes 1966088 | tf_op jit(solution)/shard_map/ppermute | solution.py:16
  249.7 206.3 %copy-start.6 = (f32[2,4,128,128]{3,2,1,0:T(8,128)S(1)}, f32[2,4,128,128]{3,2,1,0:T(8,128)}, u32[]{:S(2)}) copy-start(f32[2,4,128,128]{3,2,1,0:T(8,128)} %copy-done.5) | copy-start | bytes 1572868
  249.7 206.3 %copy-start.14 = (bf16[2,128,4,128]{3,2,1,0:T(4,128)(2,1)S(1)}, bf16[2,128,4,128]{3,2,1,0:T(4,128)(2,1)}, u32[]{:S(2)}) copy-start(bf16[2,128,4,128]{3,2,1,0:T(4,128)(2,1)} %copy-done.11) | copy-start | bytes 786436
  457.3 1.4 copy-start.10
  458.9 1.5 copy-start.15
  460.1 1.0 copy-start.18
Sparse Core Ops, SparseCore 0:
  11.8 88.4 all-gather.2
